TPU v7x, 512 devices: a whole 4x8x8 slice. The times are simulated.
512 devices in a mesh: sub: 2 (over core), row: 16 (over y, z_lo), col: 16 (over z_hi, x).
Axes of the slice: x: 4, y: 8, z: 8 (z_hi: 4, z_lo: 2; z = z_hi * 2 + z_lo), core: 2. Of those that a mesh axis runs over, the one named last changes fastest.
Arguments:
- front_entries: bfloat16 [5, 2, 16, 128, 10, 16, 128], P(None, 'sub', 'row', None, None, 'col'), may hold values from -6 to 6
- block_pattern: int32 [5, 2, 16, 10, 16], P(None, 'sub', 'row', None, 'col'), may hold values 0 or 1
- child_update: bfloat16 [2, 6, 16, 128, 6, 16, 128], P('sub', None, 'row', None, None, 'col'), may hold values from -6 to 6
- child_map: int32 [2, 6, 16], replicated, may hold values from 0 to 9, as said below
- diag_inverse: bfloat16 [1024, 1024], P('col'), may hold values from -0.0390625 to 0.0390625
Outputs:
- trailing: bfloat16 [5, 2, 16, 128, 10, 16, 128], P(None, 'sub', 'row', None, None, 'col')
Inputs may be any that keep to these rules, and one draw needn't show every extreme that they name: For each child s and each r, the 6 values child_map[s, :, r] are distinct; exactly 3 of them are even and 3 odd.
All inputs are finite; a program needn't handle non-finite values. No bound on the sum of `block_pattern` on one device may be relied on, other than what follows from the above.
Results may differ from a plain program's by a relative error of at most 0.0057.
Values may be sent and summed in bfloat16 or wider, within the bound.
A program may use at most 64 MiB of HBM per device.

v0:
```python
import jax
import jax.numpy as jnp
from jax import lax
from jax.sharding import PartitionSpec as P

PANEL = 1024


def from_partner(block, axis, apart):
    count = lax.axis_size(axis)
    route = []
    for low in range(count):
        high = low | 1 << apart
        if high != low and high < count:
            route += [(low, high), (high, low)]
    return lax.ppermute(block, axis, route)


def spread(shard, axis, root):
    mine = lax.axis_index(axis) == root
    return lax.psum(jnp.where(mine, shard, jnp.zeros_like(shard)), axis)


def place_update(update, row_targets, col_targets, sub_index, slot_count, column_count):
    wanted_rows = jnp.arange(slot_count, dtype=jnp.int32) * 2 + sub_index
    row_pick = (row_targets[None, :] == wanted_rows[:, None]).astype(jnp.bfloat16)
    col_pick = (col_targets[None, :] == jnp.arange(column_count, dtype=jnp.int32)[:, None]).astype(
        jnp.bfloat16
    )
    return jnp.einsum(
        "ak,kxly,bl->axby", row_pick, update, col_pick, preferred_element_type=jnp.float32
    )


def body(front_entries, block_pattern, child_update, child_map, diag_inverse):
    slot_count = front_entries.shape[0]
    block_size = front_entries.shape[3]
    column_count = front_entries.shape[4]
    child_count = child_update.shape[1]
    sub_index = lax.axis_index("sub")
    row_index = lax.axis_index("row")
    col_index = lax.axis_index("col")
    partner = 1 - sub_index
    own_update = child_update.reshape(child_count, block_size, child_count, block_size)
    own_maps = lax.dynamic_index_in_dim(child_map, sub_index, 0, keepdims=False)
    other_maps = lax.dynamic_index_in_dim(child_map, partner, 0, keepdims=False)
    own_rows = lax.dynamic_index_in_dim(own_maps, row_index, 1, keepdims=False)
    own_cols = lax.dynamic_index_in_dim(own_maps, col_index, 1, keepdims=False)
    other_rows = lax.dynamic_index_in_dim(other_maps, row_index, 1, keepdims=False)
    other_cols = lax.dynamic_index_in_dim(other_maps, col_index, 1, keepdims=False)
    masked = front_entries.reshape(slot_count, block_size, column_count, block_size).astype(
        jnp.float32
    )
    masked = masked * block_pattern.reshape(slot_count, 1, column_count, 1).astype(jnp.float32)
    own_part = place_update(own_update, own_rows, own_cols, sub_index, slot_count, column_count)
    received = from_partner(own_update, "sub", 0)
    partner_part = place_update(
        received, other_rows, other_cols, sub_index, slot_count, column_count
    )
    front = (masked + own_part + partner_part).astype(jnp.bfloat16)
    panel_blocks = PANEL // block_size
    col_size = lax.axis_size("col")
    panel_slots = -(-panel_blocks // col_size)
    row_total = slot_count * block_size
    piece_order = None
    leading = front[:, :, :panel_slots, None, :]
    gathered = lax.all_gather(leading, "col", axis=3, tiled=True)
    panel_matrix = gathered.reshape(row_total, panel_slots * col_size * block_size)[:, :PANEL]
    contract = (((1,), (1,)), ((), ()))
    full_inverse = lax.all_gather(diag_inverse, "col", axis=0, tiled=True)
    lower_inverse = jnp.tril(full_inverse)
    factor = lax.dot_general(
        panel_matrix, lower_inverse, contract, preferred_element_type=jnp.float32
    ).astype(jnp.bfloat16)
    column_factor = spread(factor, "row", col_index)
    both_halves = lax.all_gather(
        column_factor.reshape(slot_count, 1, block_size, PANEL), "sub", axis=1, tiled=True
    )
    column_rows = both_halves.reshape(column_count * block_size, PANEL)
    product = lax.dot_general(factor, column_rows, contract, preferred_element_type=jnp.float32)
    trailing = front.reshape(row_total, column_count * block_size).astype(jnp.float32) - product
    return trailing.astype(jnp.bfloat16).reshape(
        slot_count, 1, 1, block_size, column_count, 1, block_size
    )


def solution(mesh):
    return jax.shard_map(
        body,
        mesh=mesh,
        in_specs=(
            P(None, "sub", "row", None, None, "col", None),
            P(None, "sub", "row", None, "col"),
            P("sub", None, "row", None, None, "col", None),
            P(),
            P("col", None),
        ),
        out_specs=P(None, "sub", "row", None, None, "col", None),
        check_vma=False,
    )
```

profile of v0, /device:TPU:1, one launch (start us, length us, event | category | flops | bytes accessed | tf_op | source)
XLA Modules:
  0.0 349.8 jit_solution(13550322139019176696)
XLA Ops:
  6.5 0.0 all-gather.9.cloned.1.call-start
  6.5 8.7 %collective-permute-start = (bf16[6,128,6,128]{3,1,2,0:T(8,128)(2,1)}, bf16[6,128,6,128]{3,1,2,0:T(8,128)(2,1)S(1)}, u32[]{:S(2)}, u32[]{:S(2)}) collective-permute-start(bf16[6,128,6,128]{3,1,2,0:T(8,128)(2,1)} %bitcast.54), channel_id=1, source_target_pairs={{0,256},{256,0},{1,257},{257,1},{2,258},{258,2},{3,259},{259,3},{4... | collective-permute-start | bytes 3538952 | tf_op jit(solution)/shard_map/ppermute | solution.py:16
  15.3 1.4 dynamic-slice_reduce_fusion.2
  16.7 0.7 fusion.20
  17.4 2.2 convolution_bitcast_fusion.1
  19.6 0.0 collective-permute-done
  19.6 0.9 convolution_bitcast_fusion
  20.5 0.0 copy-start
  20.5 1.0 fusion.5
  21.5 0.5 copy-done
  22.0 2.3 fusion.2
  24.3 0.2 slice.8
  24.5 0.7 copy.32
  25.2 0.0 all-gather.9.cloned.1.call-update
  25.2 0.0 all-gather.5.cloned.1.call-start
  25.2 0.7 all-gather.5.cloned.1.call-update
  25.9 0.0 all-reduce.2.cloned.1.call-start
  26.0 67.1 %all-gather.9.cloned.1.call-done = bf16[5,128,16,128]{3,1,0,2:T(8,128)(2,1)} async-done(((bf16[5,128,1,128]{3,1,0,2:T(8,128)(2,1)}), bf16[5,128,16,128]{3,1,0,2:T(8,128)(2,1)}) %all-gather.9.cloned.1.call-update) | async-done | bytes 2621456 | tf_op jit(solution)/shard_map/all_gather | solution.py:67
  93.1 3.4 copy.33
  96.6 2.2 copy.60
  98.7 58.8 %all-gather.5.cloned.1.call-done = bf16[1024,1024]{1,0:T(8,128)(2,1)} async-done(((bf16[64,1024]{1,0:T(8,128)(2,1)}), bf16[1024,1024]{1,0:T(8,128)(2,1)}) %all-gather.5.cloned.1.call-update) | async-done | bytes 2097168 | tf_op jit(solution)/shard_map/all_gather | solution.py:70
  157.6 5.0 %broadcast_select_fusion = (bf16[640,1024]{1,0:T(8,128)(2,1)}, bf16[640,1024]{1,0:T(8,128)(2,1)}) fusion(pred[]{:T(512)S(6)} %eq.76, bf16[1024,1024]{1,0:T(8,128)(2,1)} %all-gather.5.cloned.1.call-done, bf16[640,2048]{1,0:T(8,128)(2,1)} %bitcast.53), kind=kOutput, calls=%fused_computation.20 | convolution fusion | flops 1345585152 | bytes 6029313 | tf_op jit(solution)/shard_map/dot_general | solution.py:72
  162.6 0.0 all-reduce.2.cloned.1.call-update
  162.6 0.2 all-gather.7.cloned.1.call-start
  162.9 135.2 %all-reduce.2.cloned.1.call-done = bf16[5,1,128,1024]{3,2,1,0:T(8,128)(2,1)} async-done(((bf16[5,1,128,1024]{3,2,1,0:T(8,128)(2,1)}), bf16[5,1,128,1024]{3,2,1,0:T(8,128)(2,1)}) %all-reduce.2.cloned.1.call-update) | async-done | bytes 1310736 | tf_op jit(solution)/shard_map/psum | solution.py:21
  298.1 0.0 all-gather.7.cloned.1.call-update
  298.1 2.8 copy.31
  300.9 30.7 %all-gather.7.cloned.1.call-done = bf16[5,2,128,1024]{3,2,1,0:T(8,128)(2,1)} async-done(((bf16[5,1,128,1024]{3,2,1,0:T(8,128)(2,1)}), bf16[5,2,128,1024]{3,2,1,0:T(8,128)(2,1)}) %all-gather.7.cloned.1.call-update) | async-done | bytes 2621456 | tf_op jit(solution)/shard_map/all_gather | solution.py:76
  331.5 7.3 %fusion.4 = bf16[640,1280]{1,0:T(8,128)(2,1)} fusion(bf16[640,1024]{1,0:T(8,128)(2,1)} %get-tuple-element.10, bf16[1280,1024]{1,0:T(8,128)(2,1)} %bitcast.57, f32[80,8,10,128]{3,2,1,0:T(8,128)} %bitcast.52), kind=kOutput, calls=%fused_computation.7 | convolution fusion | flops 1679360000 | bytes 8847360 | tf_op jit(solution)/shard_map/dot_general | solution.py:80
  338.8 2.8 reshape.55
  341.6 1.6 copy.35
  (1 shorter events, 0.0 us)
Async XLA Ops:
  6.5 86.6 %all-gather.9.cloned.1.call-start = ((), (), s32[]{:S(2)}) async-start(), calls=%async_computation.3 | async-start | bytes 2785280 | tf_op jit(solution)/shard_map/all_gather | solution.py:67
  6.5 13.1 %collective-permute-start = (bf16[6,128,6,128]{3,1,2,0:T(8,128)(2,1)}, bf16[6,128,6,128]{3,1,2,0:T(8,128)(2,1)S(1)}, u32[]{:S(2)}, u32[]{:S(2)}) collective-permute-start(bf16[6,128,6,128]{3,1,2,0:T(8,128)(2,1)} %bitcast.54), channel_id=1, source_target_pairs={{0,256},{256,0},{1,257},{257,1},{2,258},{258,2},{3,259},{259,3},{4... | collective-permute-start | bytes 3538952 | tf_op jit(solution)/shard_map/ppermute | solution.py:16
  20.5 1.4 copy-start
  25.2 132.4 %all-gather.5.cloned.1.call-start = ((), (), s32[]{:S(2)}) async-start(), calls=%async_computation | async-start | bytes 2228224 | tf_op jit(solution)/shard_map/all_gather | solution.py:70
  25.9 272.2 %all-reduce.2.cloned.1.call-start = ((), (), s32[]{:S(2)}) async-start(), calls=%async_computation.1 | async-start | bytes 2621440 | tf_op jit(solution)/shard_map/psum | solution.py:21
  162.6 168.9 %all-gather.7.cloned.1.call-start = ((), (), s32[]{:S(2)}) async-start(), calls=%async_computation.2 | async-start | bytes 3932160 | tf_op jit(solution)/shard_map/all_gather | solution.py:76
Sparse Core Ops, SparseCore 0:
  25.3 67.7 all-gather.8
  96.1 61.3 all-gather.4
  162.8 135.2 all-reduce.1
  300.0 31.4 all-gather.6
where the time goes:
time: 350 us
  waiting for transfers between devices  293 us (84%)
  matrix products  18.6 us (5%)
  local copies, waits for them, and re-layouts  15.6 us (4%)
  between operations  13.2 us (4%)
  starting transfers between devices  9.04 us (3%)
    psum x1, waiting for transfers between devices, spread(): return lax.psum(jnp.where(mine, shard, jnp.zeros_like(shard)), axis)  135 us
    all_gather x1, waiting for transfers between devices, body(): gathered = lax.all_gather(leading, 'col', axis=3, tiled=True)  67.1 us
    all_gather x1, waiting for transfers between devices, body(): full_inverse = lax.all_gather(diag_inverse, 'col', axis=0, tiled=True)  58.8 us
    all_gather x1, waiting for transfers between devices, body(): lax.all_gather(column_factor.reshape(slot_count, 1, block_size, PANEL), '...  30.7 us
    ppermute x1, starting transfers between devices, from_partner(): return lax.ppermute(block, axis, route)  8.74 us
    dot_general x1, matrix products, body(): lax.dot_general(factor, column_rows, contract, preferred_element_type=jnp...  7.25 us
  transfers between devices with their start and end apart: 5, of which 4 were waited for; matrix products, arithmetic and copies ran while one was open for 4% of the time, Pallas kernels for 0%

commit v1 on v0

v1 whole, which is shorter than its diff:
```python
import jax
import jax.numpy as jnp
from jax import lax
from jax.experimental import pallas as pl
from jax.experimental.pallas import tpu as pltpu
from jax.sharding import PartitionSpec as P

MESH = pl.DeviceIdType.MESH
F32 = jnp.float32
BF16 = jnp.bfloat16

BLK = 128
RBK = 5
MB = 10
CBK = 6
ROWS = RBK * BLK
PANEL = 1024
PIECES = 4
PR = ROWS // PIECES
NT = (((1,), (1,)), ((), ()))


def bitrev3(value):
    return (value % 2) * 4 + ((value // 2) % 2) * 2 + value // 4


def kernel(
    cmap, pattern, entries_hbm, child_hbm, inverse_hbm, out_hbm,
    child, entries, front, pack0, pack, got0, got, left, right, inv, diag, fleft, fright, outv,
    local_sem, pk_send, pk_recv, lz_send, lz_recv, lx_send, lx_recv, lp_sem,
    sc_send, sc_recv, pr_send, pr_recv, z_send, z_recv, x_send, x_recv,
    y_send, y_recv, h_send, h_recv, out_sem,
):
    s = lax.axis_index("sub")
    row = lax.axis_index("row")
    col = lax.axis_index("col")
    y, zl = row // 2, row % 2
    zh, x = col // 4, col % 4
    holder = zh < 2
    other = 1 - s

    def at_row(r):
        return {"row": r}

    def at_col(c):
        return {"col": c}

    mate = {"sub": other}
    z_up, z_down = at_col(((zh + 1) % 4) * 4 + x), at_col(((zh + 3) % 4) * 4 + x)
    z_swap = at_col((zh + 1 - 2 * (zh % 2)) * 4 + x)
    z_flip = at_col((3 - zh) * 4 + x)
    x_up, x_down = at_col(zh * 4 + (x + 1) % 4), at_col(zh * 4 + (x + 3) % 4)
    y_up, y_down = at_row(((y + 1) % 8) * 2 + zl), at_row(((y + 7) % 8) * 2 + zl)
    pair = at_row(y * 2 + 1 - zl)

    def slot_of(y_at, group):
        return bitrev3((y_at + 24 - 3 * (group // 2) - 6) % 8)

    send_y = (bitrev3(col % 8) + 3 * y + 6) % 8
    source = {"row": col, "col": slot_of(y, col)}

    def rdma(src, dst, send, recv, to):
        return pltpu.make_async_remote_copy(
            src_ref=src, dst_ref=dst, send_sem=send, recv_sem=recv, device_id=to, device_id_type=MESH
        )

    def landed(dst, send, recv):
        rdma(dst, dst, send, recv, mate).wait_recv()

    def each(n, fn):
        def step(i, carry):
            fn(i)
            return carry

        lax.fori_loop(0, n, step, 0)

    child_in = pltpu.make_async_copy(child_hbm, child, local_sem.at[0])
    entries_in = pltpu.make_async_copy(entries_hbm, entries, local_sem.at[1])
    inv_in = pltpu.make_async_copy(
        inverse_hbm.at[pl.ds(pl.multiple_of(s * 32, 32), 32)], inv.at[zh, x, s], local_sem.at[2]
    )
    child_in.start()
    inv_in.start()
    entries_in.start()

    barrier = pltpu.get_barrier_semaphore()
    for to in (mate, z_up, z_down, x_up, x_down, y_up, y_down, pair, source):
        pl.semaphore_signal(barrier, inc=1, device_id=to, device_id_type=MESH)

    own_row = [cmap[a, s, row] for a in range(CBK)]
    other_row = [cmap[a, other, row] for a in range(CBK)]

    def nth_rows(values, parity):
        found = [jnp.int32(0)] * 3
        count = jnp.int32(0)
        for a in range(CBK):
            hit = values[a] % 2 == parity
            for n in range(3):
                found[n] = jnp.where(hit & (count == n), jnp.int32(a), found[n])
            count = count + jnp.where(hit, jnp.int32(1), jnp.int32(0))
        return found

    def lookup(values, wanted):
        index, have = jnp.int32(0), jnp.float32(0)
        for n, value in enumerate(values):
            index = jnp.where(value == wanted, jnp.int32(n), index)
            have = jnp.where(value == wanted, jnp.float32(1), have)
        return index, have

    out_rows = nth_rows(own_row, other)
    own_cols = [cmap[b, s, col] for b in range(CBK)]
    first_col, _ = lookup(own_cols, jnp.int32(0))
    child_in.wait()
    for n in range(3):
        pack0[n] = child[out_rows[n], first_col]
        for b in range(CBK):
            pack[n, b] = child[out_rows[n], b]

    in_slots = [jnp.int32(-1)] * 3
    count = jnp.int32(0)
    for a in range(CBK):
        hit = other_row[a] % 2 == s
        for n in range(3):
            in_slots[n] = jnp.where(hit & (count == n), other_row[a], in_slots[n])
        count = count + jnp.where(hit, jnp.int32(1), jnp.int32(0))
    own_at = [lookup(own_row, 2 * k + s) for k in range(RBK)]
    other_at = [lookup(in_slots, 2 * k + s) for k in range(RBK)]

    inv_in.wait()
    pl.semaphore_wait(barrier, 8 + jnp.where(holder, 2, 0))

    pk0_copy = rdma(pack0, got0, pk_send.at[0], pk_recv.at[0], mate)
    pk_copy = rdma(pack, got, pk_send.at[1], pk_recv.at[1], mate)
    pk0_copy.start()
    pk_copy.start()

    mine = inv.at[zh, x, s]
    z_below, z_above, z_far = (zh + 3) % 4, (zh + 1) % 4, (zh + 2) % 4
    lz_up = rdma(mine, mine, lz_send.at[0], lz_recv.at[0], z_up)
    lz_down = rdma(mine, mine, lz_send.at[1], lz_recv.at[1], z_down)
    lz_up.start()
    lz_down.start()
    low_half = inv.at[z_below, x, s, pl.ds(0, 16)]
    high_half = inv.at[z_above, x, s, pl.ds(16, 16)]
    lz_up2 = rdma(low_half, low_half, lz_send.at[2], lz_recv.at[2], z_up)
    lz_down2 = rdma(high_half, high_half, lz_send.at[3], lz_recv.at[3], z_down)

    def block(k, m, own_b, own_f, theirs, theirs_f):
        a, have_a = own_at[k]
        n, have_n = other_at[k]
        scale = pattern[k, m].astype(F32)
        value = entries[k, m].astype(F32) * scale
        value = value + child[a, own_b].astype(F32) * (have_a * own_f)
        return (value + theirs(n).astype(F32) * (have_n * theirs_f)).astype(BF16)

    def columns(m):
        own_b, own_f = lookup([cmap[b, s, col] for b in range(CBK)], m)
        other_b, other_f = lookup([cmap[b, other, col] for b in range(CBK)], m)
        return own_b, own_f, other_b, other_f

    entries_in.wait()
    landed(got0, pk_send.at[0], pk_recv.at[0])

    first = jnp.where((zh == 1) | (zh == 2), 1, 0)
    slot_a = first * 4 + x
    slot_b = (1 - first) * 4 + x

    def piece(p):
        return pl.ds(pl.multiple_of(p * PR, 32), PR)

    def z_copy(which, p):
        ref = left.at[slot_a, piece(p)]
        if which == 0:
            return rdma(ref, ref, z_send.at[0, p], z_recv.at[0, p], z_swap)
        if which == 1:
            return rdma(ref, ref, z_send.at[1, p], z_recv.at[0, p], z_flip)
        return rdma(ref, ref, z_send.at[0, p], z_recv.at[1, p], z_swap)

    def x_copy(which, p):
        x_below, x_above = (x + 3) % 4, (x + 1) % 4
        slot, to = [
            (slot_a, x_up),
            (slot_a, x_down),
            (slot_b, x_up),
            (slot_b, x_down),
            (first * 4 + x_below, x_up),
            ((1 - first) * 4 + x_above, x_down),
        ][which]
        ref = left.at[slot, piece(p)]
        return rdma(ref, ref, x_send.at[which, p], x_recv.at[which, p], to)

    def x_landed(which, p):
        slot = [
            first * 4 + (x + 3) % 4,
            first * 4 + (x + 1) % 4,
            (1 - first) * 4 + (x + 3) % 4,
            (1 - first) * 4 + (x + 1) % 4,
            first * 4 + (x + 2) % 4,
            (1 - first) * 4 + (x + 2) % 4,
        ][which]
        landed(left.at[slot, piece(p)], x_send.at[which, p], x_recv.at[which, p])

    def scatter_copy(half, p):
        part = piece(2 * half + p)
        return rdma(
            left.at[slot_a, part], right.at[s, slot_a, part], sc_send.at[half, p], sc_recv.at[p],
            {"row": send_y * 2 + half, "col": row},
        )

    @pl.when(holder)
    def _():
        own_b, own_f, other_b, other_f = columns(jnp.int32(0))
        for k in range(RBK):
            left[slot_a, pl.ds(k * BLK, BLK)] = block(k, 0, own_b, own_f, lambda n: got0[n], other_f)

        def go(p):
            scatter_copy(0, p).start()
            scatter_copy(1, p).start()

        each(2, go)

        def go_left(p):
            z_copy(0, p).start()
            z_copy(1, p).start()
            x_copy(0, p).start()
            x_copy(1, p).start()

        each(PIECES, go_left)

    landed(inv.at[z_below, x, s], lz_send.at[0], lz_recv.at[0])
    lz_up2.start()
    landed(inv.at[z_above, x, s], lz_send.at[1], lz_recv.at[1])
    lz_down2.start()

    def a_here(p):
        landed(left.at[slot_a, piece(p)], z_send.at[0, p], z_recv.at[0, p])

    @pl.when(jnp.logical_not(holder))
    def _():
        def go(p):
            a_here(p)
            z_copy(2, p).start()
            x_copy(0, p).start()
            x_copy(1, p).start()

        each(PIECES, go)

    far = inv.at[z_far, x, s]
    landed(far.at[pl.ds(0, 16)], lz_send.at[2], lz_recv.at[2])
    landed(far.at[pl.ds(16, 16)], lz_send.at[3], lz_recv.at[3])

    def inv_group(group, x_at):
        if group == 0:
            return inv.at[pl.ds(0, 2), x_at, s, :, pl.ds(0, PANEL // 2)]
        return inv.at[pl.ds(2, 2), x_at, s]

    def lx_copy(which):
        group, x_at, to = [
            (0, x, x_up),
            (0, x, x_down),
            (1, x, x_up),
            (1, x, x_down),
            (0, (x + 3) % 4, x_up),
            (1, (x + 1) % 4, x_down),
        ][which]
        ref = inv_group(group, x_at)
        return rdma(ref, ref, lx_send.at[which], lx_recv.at[which], to)

    def lx_landed(which):
        group, x_at = [
            (0, (x + 3) % 4),
            (0, (x + 1) % 4),
            (1, (x + 3) % 4),
            (1, (x + 1) % 4),
            (0, (x + 2) % 4),
            (1, (x + 2) % 4),
        ][which]
        landed(inv_group(group, x_at), lx_send.at[which], lx_recv.at[which])

    for which in range(4):
        lx_copy(which).start()

    own_slot = slot_of(y, col)

    def turn(q):
        return (2 * zl + q) % 4

    def y_copy(up, d, q):
        slot = slot_of((y + 8 - (d - 1)) % 8 if up else (y + d - 1) % 8, col)
        ref = right.at[s, slot, piece(turn(q))]
        way = 0 if up else 1
        return rdma(
            ref, ref, y_send.at[way, d - 1, q], y_recv.at[way, d - 1, q], y_up if up else y_down
        )

    def y_landed(up, d, q):
        slot = slot_of((y + 8 - d) % 8 if up else (y + d) % 8, col)
        way = 0 if up else 1
        landed(
            right.at[s, slot, piece(turn(q))], y_send.at[way, d - 1, q], y_recv.at[way, d - 1, q]
        )

    def pair_copy(p):
        ref = right.at[s, own_slot, piece(2 * zl + p)]
        return rdma(ref, ref, pr_send.at[p], pr_recv.at[p], pair)

    def hand_copy(which):
        shift = [0, 7, 1, 6, 2, 5, 3][which]
        ref = right.at[s, slot_of((y + shift) % 8, col)]
        return rdma(ref, ref, h_send.at[which], h_recv.at[which], mate)

    def hand_half(which):
        half = (zl + which) % 2
        ref = right.at[s, slot_of((y + 4) % 8, col), pl.ds(pl.multiple_of(half * 2 * PR, 32), 2 * PR)]
        return rdma(ref, ref, h_send.at[7 + which], h_recv.at[7 + which], mate)

    def from_source(p):
        landed(right.at[s, own_slot, piece(2 * zl + p)], sc_send.at[0, p], sc_recv.at[p])
        pair_copy(p).start()
        y_copy(True, 1, p).start()
        y_copy(False, 1, p).start()

    each(2, from_source)

    def assemble(m):
        own_b, own_f, other_b, other_f = columns(m)
        for k in range(RBK):
            front[k, m] = block(k, m, own_b, own_f, lambda n: got[n, other_b], other_f)

    landed(got, pk_send.at[1], pk_recv.at[1])
    each(RBK, assemble)

    def b_ready(p):
        @pl.when(holder)
        def _():
            landed(left.at[slot_b, piece(p)], z_send.at[0, p], z_recv.at[0, p])

        @pl.when(jnp.logical_not(holder))
        def _():
            landed(left.at[slot_b, piece(p)], z_send.at[0, p], z_recv.at[1, p])

        x_copy(2, p).start()
        x_copy(3, p).start()

    each(PIECES, b_ready)

    def from_pair(p):
        landed(right.at[s, own_slot, piece(2 * (1 - zl) + p)], pr_send.at[p], pr_recv.at[p])
        y_copy(True, 1, p + 2).start()
        y_copy(False, 1, p + 2).start()

    each(2, from_pair)
    hand_copy(0).start()

    def x_pass(p):
        x_landed(0, p)
        x_copy(4, p).start()
        x_landed(3, p)
        x_copy(5, p).start()

    each(PIECES, x_pass)

    lx_landed(0)
    lx_copy(4).start()
    lx_landed(3)
    lx_copy(5).start()

    def y_pass(d):
        def go(q):
            y_landed(True, d, q)
            y_copy(True, d + 1, q).start()
            y_landed(False, d, q)
            y_copy(False, d + 1, q).start()

        return go

    each(PIECES, y_pass(1))
    hand_copy(1).start()
    hand_copy(2).start()

    each(RBK, lambda m: assemble(m + RBK))

    def x_rest(p):
        for which in (2, 1, 4, 5):
            x_landed(which, p)

    each(PIECES, x_rest)
    for which in (2, 1, 4, 5):
        lx_landed(which)
    inv_hand = rdma(inv.at[:, :, s], inv.at[:, :, s], lp_sem.at[0], lp_sem.at[1], mate)
    inv_hand.start()

    each(PIECES, y_pass(2))
    hand_copy(3).start()
    hand_copy(4).start()

    landed(inv.at[:, :, other], lp_sem.at[0], lp_sem.at[1])
    keep = lax.broadcasted_iota(jnp.int32, (256, 256), 0) >= lax.broadcasted_iota(jnp.int32, (256, 256), 1)
    for nb in range(4):
        tile = inv[nb, :, :, :, pl.ds(nb * 256, 256)].reshape(256, 256).astype(F32)
        diag[nb] = jnp.where(keep, tile, 0.0).astype(BF16)

    def weights(nb):
        if nb == 0:
            return diag[0]
        return jnp.concatenate(
            [inv[nb, :, :, :, pl.ds(0, nb * 256)].reshape(256, nb * 256), diag[nb]], axis=1
        )

    def y_last(q):
        y_landed(True, 3, q)
        y_copy(True, 4, q).start()
        y_landed(False, 3, q)

    def y_last2(q):
        y_landed(True, 3, q + 2)
        y_landed(False, 3, q + 2)
        y_copy(False, 4, q + 2).start()

    each(2, y_last)
    each(2, y_last2)
    hand_copy(5).start()
    hand_copy(6).start()

    def left_factor(t):
        part = pl.ds(pl.multiple_of(t * 320, 64), 320)
        for nb in range(4):
            lhs = jnp.concatenate([left[c, part] for c in range(2 * nb + 2)], axis=1)
            fleft[part, pl.ds(nb * 256, 256)] = lax.dot_general(
                lhs, weights(nb), NT, preferred_element_type=F32
            ).astype(BF16)

    each(2, left_factor)

    each(2, lambda q: y_landed(True, 4, q))
    hand_half(0).start()
    each(2, lambda q: y_landed(False, 4, q + 2))
    hand_half(1).start()

    for which, shift in enumerate([0, 7, 1, 6, 2, 5, 3]):
        landed(right.at[other, slot_of((y + shift) % 8, col)], h_send.at[which], h_recv.at[which])
    for which in range(2):
        half = (zl + which) % 2
        landed(
            right.at[other, slot_of((y + 4) % 8, col), pl.ds(pl.multiple_of(half * 2 * PR, 32), 2 * PR)],
            h_send.at[7 + which], h_recv.at[7 + which],
        )

    def out_copy(kk):
        cols = pl.ds(2 * kk, 2)
        return pltpu.make_async_copy(outv.at[:, cols], out_hbm.at[:, cols], out_sem.at[kk])

    def finish(kk):
        part = pl.ds(pl.multiple_of(kk * BLK, BLK), BLK)
        for nb in range(4):
            lhs = jnp.concatenate(
                [
                    jnp.concatenate([right[h, c, part] for c in range(2 * nb + 2)], axis=1)
                    for h in range(2)
                ],
                axis=0,
            )
            fright[:, pl.ds(nb * 256, 256)] = lax.dot_general(
                lhs, weights(nb), NT, preferred_element_type=F32
            ).astype(BF16)
        product = lax.dot_general(fleft[...], fright[...], NT, preferred_element_type=F32)
        for k in range(RBK):
            for h in range(2):
                tile = product[k * BLK:(k + 1) * BLK, h * BLK:(h + 1) * BLK]
                outv[k, 2 * kk + h] = (front[k, 2 * kk + h].astype(F32) - tile).astype(BF16)
        out_copy(kk).start()

    each(RBK, finish)
    each(RBK, lambda kk: out_copy(kk).wait())

    pk0_copy.wait_send()
    pk_copy.wait_send()
    for copy in (lz_up, lz_down, lz_up2, lz_down2, inv_hand):
        copy.wait_send()
    for which in range(6):
        lx_copy(which).wait_send()

    @pl.when(holder)
    def _():
        def done(p):
            scatter_copy(0, p).wait_send()
            scatter_copy(1, p).wait_send()

        each(2, done)

    def left_done(p):
        z_copy(0, p).wait_send()

        @pl.when(holder)
        def _():
            z_copy(1, p).wait_send()

        for which in range(6):
            x_copy(which, p).wait_send()
        for d in range(1, 4):
            y_copy(True, d, p).wait_send()
            y_copy(False, d, p).wait_send()

    each(PIECES, left_done)

    def last_done(p):
        pair_copy(p).wait_send()
        y_copy(True, 4, p).wait_send()
        y_copy(False, 4, p + 2).wait_send()

    each(2, last_done)
    for which in range(7):
        hand_copy(which).wait_send()
    for which in range(2):
        hand_half(which).wait_send()


def body(front_entries, block_pattern, child_update, child_map, diag_inverse):
    entries = front_entries.transpose(0, 4, 1, 2, 5, 3, 6).reshape(RBK, MB, BLK, BLK)
    child = child_update.transpose(0, 1, 4, 2, 5, 3, 6).reshape(CBK, CBK, BLK, BLK)
    pattern = block_pattern.reshape(RBK, MB)
    cmap = child_map.transpose(1, 0, 2)
    smem = pl.BlockSpec(memory_space=pltpu.SMEM)
    anyspace = pl.BlockSpec(memory_space=pl.ANY)
    dma = pltpu.SemaphoreType.DMA
    out = pl.pallas_call(
        kernel,
        out_shape=jax.ShapeDtypeStruct((RBK, MB, BLK, BLK), BF16),
        in_specs=[smem, smem, anyspace, anyspace, anyspace],
        out_specs=anyspace,
        scratch_shapes=[
            pltpu.VMEM((CBK, CBK, BLK, BLK), BF16),
            pltpu.VMEM((RBK, MB, BLK, BLK), BF16),
            pltpu.VMEM((RBK, MB, BLK, BLK), BF16),
            pltpu.VMEM((3, BLK, BLK), BF16),
            pltpu.VMEM((3, CBK, BLK, BLK), BF16),
            pltpu.VMEM((3, BLK, BLK), BF16),
            pltpu.VMEM((3, CBK, BLK, BLK), BF16),
            pltpu.VMEM((8, ROWS, BLK), BF16),
            pltpu.VMEM((2, 8, ROWS, BLK), BF16),
            pltpu.VMEM((4, 4, 2, 32, PANEL), BF16),
            pltpu.VMEM((4, 256, 256), BF16),
            pltpu.VMEM((ROWS, PANEL), BF16),
            pltpu.VMEM((2 * BLK, PANEL), BF16),
            pltpu.VMEM((RBK, MB, BLK, BLK), BF16),
            dma((3,)),
            dma((2,)), dma((2,)),
            dma((4,)), dma((4,)),
            dma((6,)), dma((6,)),
            dma((2,)),
            dma((2, 2)), dma((2,)),
            dma((2,)), dma((2,)),
            dma((2, PIECES)), dma((2, PIECES)),
            dma((6, PIECES)), dma((6, PIECES)),
            dma((2, 4, PIECES)), dma((2, 4, PIECES)),
            dma((9,)), dma((9,)),
            dma((RBK,)),
        ],
        compiler_params=pltpu.CompilerParams(
            collective_id=0, has_side_effects=True, vmem_limit_bytes=48 * 1024 * 1024
        ),
    )(cmap, pattern, entries, child, diag_inverse)
    out = out.reshape(RBK, MB, 1, 1, 1, BLK, BLK)
    return out.transpose(0, 2, 3, 5, 1, 4, 6)


def solution(mesh):
    return jax.shard_map(
        body,
        mesh=mesh,
        in_specs=(
            P(None, "sub", "row", None, None, "col", None),
            P(None, "sub", "row", None, "col"),
            P("sub", None, "row", None, None, "col", None),
            P(),
            P("col", None),
        ),
        out_specs=P(None, "sub", "row", None, None, "col", None),
        check_vma=False,
    )
```

time: 350 us -> 73.8 us (0.21)
  waiting for transfers between devices: 293 us -> 0 us
  Pallas kernels: 0 us -> 67.4 us
  matrix products: 18.6 us -> 0 us
  between operations: 13.2 us -> 0.01 us
  local copies, waits for them, and re-layouts: 15.6 us -> 6.15 us
  starting transfers between devices: 9.04 us -> 0 us
    all_gather x3 -> x0, waiting for transfers between devices: 157 us -> none  [the longest x1 67.1 us: body(): gathered = lax.all_gather(leading, 'col', axis=3, tiled=True)]
    psum x1 -> x0, waiting for transfers between devices: 135 us -> none  [spread(): return lax.psum(jnp.where(mine, shard, jnp.zeros_like(shard)), axis)]
    pallas_call x0 -> x1, Pallas kernels: none -> 67.4 us  [body(): pl.pallas_call(kernel, out_shape=jax.ShapeDtypeStruct((RBK, MB, BLK, BLK)...]
    dot_general x6 -> x0, matrix products: 18.6 us -> none  [the longest x1 7.25 us: body(): lax.dot_general(factor, column_rows, contract, preferred_element_type=jnp...]
    ppermute x1 -> x0, starting transfers between devices: 8.74 us -> none  [from_partner(): return lax.ppermute(block, axis, route)]
    reshape x2 -> x0, local copies, waits for them, and re-layouts: 4.41 us -> none  [body(): trailing.astype(jnp.bfloat16)]
  transfers between devices with their start and end apart: 5 -> 0, of which waited for: 4 -> 0; matrix products, arithmetic and copies ran while one was open for 4% -> 0% of each run, Pallas kernels for 0% -> 0%
where the time goes in v1:
time: 73.8 us; the launch traced here: 73.5 us
  Pallas kernels  67.4 us (91%)
  local copies, waits for them, and re-layouts  6.15 us (8%)
    pallas_call x1, Pallas kernels, body(): pl.pallas_call(kernel, out_shape=jax.ShapeDtypeStruct((RBK, MB, BLK, BLK)...  67.4 us
    unnamed x10, local copies, waits for them, and re-layouts  6.15 us

profile of v1, /device:TPU:1, one launch (start us, length us, event | category | flops | bytes accessed | tf_op | source)
XLA Modules:
  0.0 73.5 jit_solution(5663032131996441551)
XLA Ops:
  0.0 0.7 copy.11
  0.7 0.0 copy-start
  0.7 1.4 %copy-done = bf16[5,1,1,128,10,1,128]{6,3,5,4,2,1,0:T(8,128)(2,1)S(1)} copy-done((bf16[5,1,1,128,10,1,128]{6,3,5,4,2,1,0:T(8,128)(2,1)S(1)}, bf16[5,1,1,128,10,1,128]{6,3,5,4,2,1,0:T(8,128)(2,1)}, u32[]{:S(2)}) %copy-start) | copy-done | bytes 1638424
  2.1 0.0 copy-start.1
  2.1 1.3 %copy-done.1 = bf16[1,6,1,128,6,1,128]{6,3,5,4,2,1,0:T(8,128)(2,1)S(1)} copy-done((bf16[1,6,1,128,6,1,128]{6,3,5,4,2,1,0:T(8,128)(2,1)S(1)}, bf16[1,6,1,128,6,1,128]{6,3,5,4,2,1,0:T(8,128)(2,1)}, u32[]{:S(2)}) %copy-start.1) | copy-done | bytes 1179672
  3.4 0.0 copy-start.2
  3.4 0.9 %copy-done.2 = bf16[64,1024]{1,0:T(8,128)(2,1)S(1)} copy-done((bf16[64,1024]{1,0:T(8,128)(2,1)S(1)}, bf16[64,1024]{1,0:T(8,128)(2,1)}, u32[]{:S(2)}) %copy-start.2) | copy-done | bytes 131096
  4.3 0.0 copy-start.3
  4.3 0.7 copy-done.3
  5.0 67.4 %shard_map.55 = bf16[5,10,128,128]{3,2,1,0:T(8,128)(2,1)S(1)} custom-call(s32[6,2,16]{2,1,0:T(2,128)S(1)} %bitcast.23, s32[5,10]{1,0:T(8,128)S(1)} %bitcast.22, bf16[5,10,128,128]{3,2,1,0:T(8,128)(2,1)S(1)} %bitcast.20, bf16[6,6,128,128]{3,2,1,0:T(8,128)(2,1)S(1)} %bitcast.21, bf16[64,1024]{1,0:T(8,128)(2,1)S(1)} %copy-done.2), custom_call_target="tpu_custom_call" | custom-call | tf_op jit(solution)/shard_map/pallas_call | solution.py:526
  72.4 1.2 %copy.13 = bf16[5,1,1,128,10,1,128]{6,3,5,4,2,1,0:T(8,128)(2,1)} copy(bf16[5,1,1,128,10,1,128]{6,3,5,4,2,1,0:T(8,128)(2,1)S(1)} %bitcast.19) | data formatting | bytes 3276800
Async XLA Ops:
  0.7 1.4 %copy-start = (bf16[5,1,1,128,10,1,128]{6,3,5,4,2,1,0:T(8,128)(2,1)S(1)}, bf16[5,1,1,128,10,1,128]{6,3,5,4,2,1,0:T(8,128)(2,1)}, u32[]{:S(2)}) copy-start(bf16[5,1,1,128,10,1,128]{6,3,5,4,2,1,0:T(8,128)(2,1)} %param.5) | copy-start | bytes 4915204
  2.1 1.3 %copy-start.1 = (bf16[1,6,1,128,6,1,128]{6,3,5,4,2,1,0:T(8,128)(2,1)S(1)}, bf16[1,6,1,128,6,1,128]{6,3,5,4,2,1,0:T(8,128)(2,1)}, u32[]{:S(2)}) copy-start(bf16[1,6,1,128,6,1,128]{6,3,5,4,2,1,0:T(8,128)(2,1)} %param.7) | copy-start | bytes 3538948
  3.4 0.9 %copy-start.2 = (bf16[64,1024]{1,0:T(8,128)(2,1)S(1)}, bf16[64,1024]{1,0:T(8,128)(2,1)}, u32[]{:S(2)}) copy-start(bf16[64,1024]{1,0:T(8,128)(2,1)} %inverse_hbm.1) | copy-start | bytes 393220
  4.3 0.7 copy-start.3

commit v2 on v1

--- a/solution.py
+++ b/solution.py
@@ -25,9 +25,10 @@
 
 
 def kernel(
-    cmap, pattern, entries_hbm, child_hbm, inverse_hbm, out_hbm,
+    cmap_hbm, pattern_hbm, entries_hbm, child_hbm, inverse_hbm, out_hbm,
+    cmap, pattern,
     child, entries, front, pack0, pack, got0, got, left, right, inv, diag, fleft, fright, outv,
-    local_sem, pk_send, pk_recv, lz_send, lz_recv, lx_send, lx_recv, lp_sem,
+    local_sem, pk_send, pk_recv, lz_send, lz_recv, lx_send, lx_recv, lp_send, lp_recv,
     sc_send, sc_recv, pr_send, pr_recv, z_send, z_recv, x_send, x_recv,
     y_send, y_recv, h_send, h_recv, out_sem,
 ):
@@ -79,14 +80,19 @@
     inv_in = pltpu.make_async_copy(
         inverse_hbm.at[pl.ds(pl.multiple_of(s * 32, 32), 32)], inv.at[zh, x, s], local_sem.at[2]
     )
+    cmap_in = pltpu.make_async_copy(cmap_hbm, cmap, local_sem.at[3])
+    pattern_in = pltpu.make_async_copy(pattern_hbm, pattern, local_sem.at[4])
+    cmap_in.start()
     child_in.start()
     inv_in.start()
+    pattern_in.start()
     entries_in.start()
 
     barrier = pltpu.get_barrier_semaphore()
     for to in (mate, z_up, z_down, x_up, x_down, y_up, y_down, pair, source):
         pl.semaphore_signal(barrier, inc=1, device_id=to, device_id_type=MESH)
 
+    cmap_in.wait()
     own_row = [cmap[a, s, row] for a in range(CBK)]
     other_row = [cmap[a, other, row] for a in range(CBK)]
 
@@ -131,8 +137,6 @@
 
     pk0_copy = rdma(pack0, got0, pk_send.at[0], pk_recv.at[0], mate)
     pk_copy = rdma(pack, got, pk_send.at[1], pk_recv.at[1], mate)
-    pk0_copy.start()
-    pk_copy.start()
 
     mine = inv.at[zh, x, s]
     z_below, z_above, z_far = (zh + 3) % 4, (zh + 1) % 4, (zh + 2) % 4
@@ -145,10 +149,13 @@
     lz_up2 = rdma(low_half, low_half, lz_send.at[2], lz_recv.at[2], z_up)
     lz_down2 = rdma(high_half, high_half, lz_send.at[3], lz_recv.at[3], z_down)
 
+    pk0_copy.start()
+    pk_copy.start()
+
     def block(k, m, own_b, own_f, theirs, theirs_f):
         a, have_a = own_at[k]
         n, have_n = other_at[k]
-        scale = pattern[k, m].astype(F32)
+        scale = pattern[k, 0, m].astype(F32)
         value = entries[k, m].astype(F32) * scale
         value = value + child[a, own_b].astype(F32) * (have_a * own_f)
         return (value + theirs(n).astype(F32) * (have_n * theirs_f)).astype(BF16)
@@ -158,6 +165,7 @@
         other_b, other_f = lookup([cmap[b, other, col] for b in range(CBK)], m)
         return own_b, own_f, other_b, other_f
 
+    pattern_in.wait()
     entries_in.wait()
     landed(got0, pk_send.at[0], pk_recv.at[0])
 
@@ -207,78 +215,28 @@
             {"row": send_y * 2 + half, "col": row},
         )
 
-    @pl.when(holder)
-    def _():
-        own_b, own_f, other_b, other_f = columns(jnp.int32(0))
-        for k in range(RBK):
-            left[slot_a, pl.ds(k * BLK, BLK)] = block(k, 0, own_b, own_f, lambda n: got0[n], other_f)
-
-        def go(p):
-            scatter_copy(0, p).start()
-            scatter_copy(1, p).start()
-
-        each(2, go)
-
-        def go_left(p):
-            z_copy(0, p).start()
-            z_copy(1, p).start()
-            x_copy(0, p).start()
-            x_copy(1, p).start()
-
-        each(PIECES, go_left)
-
-    landed(inv.at[z_below, x, s], lz_send.at[0], lz_recv.at[0])
-    lz_up2.start()
-    landed(inv.at[z_above, x, s], lz_send.at[1], lz_recv.at[1])
-    lz_down2.start()
-
     def a_here(p):
         landed(left.at[slot_a, piece(p)], z_send.at[0, p], z_recv.at[0, p])
 
-    @pl.when(jnp.logical_not(holder))
-    def _():
-        def go(p):
-            a_here(p)
-            z_copy(2, p).start()
-            x_copy(0, p).start()
-            x_copy(1, p).start()
-
-        each(PIECES, go)
-
     far = inv.at[z_far, x, s]
-    landed(far.at[pl.ds(0, 16)], lz_send.at[2], lz_recv.at[2])
-    landed(far.at[pl.ds(16, 16)], lz_send.at[3], lz_recv.at[3])
-
-    def inv_group(group, x_at):
-        if group == 0:
-            return inv.at[pl.ds(0, 2), x_at, s, :, pl.ds(0, PANEL // 2)]
-        return inv.at[pl.ds(2, 2), x_at, s]
-
-    def lx_copy(which):
-        group, x_at, to = [
-            (0, x, x_up),
-            (0, x, x_down),
-            (1, x, x_up),
-            (1, x, x_down),
-            (0, (x + 3) % 4, x_up),
-            (1, (x + 1) % 4, x_down),
-        ][which]
-        ref = inv_group(group, x_at)
-        return rdma(ref, ref, lx_send.at[which], lx_recv.at[which], to)
-
-    def lx_landed(which):
-        group, x_at = [
-            (0, (x + 3) % 4),
-            (0, (x + 1) % 4),
-            (1, (x + 3) % 4),
-            (1, (x + 1) % 4),
-            (0, (x + 2) % 4),
-            (1, (x + 2) % 4),
-        ][which]
-        landed(inv_group(group, x_at), lx_send.at[which], lx_recv.at[which])
-
-    for which in range(4):
-        lx_copy(which).start()
+
+    def inv_part(zq, x_at):
+        return inv.at[zq, x_at, s, :, pl.ds(0, (zq + 1) * 256)]
+
+    def lx_copy(kind, zq):
+        if kind < 2:
+            x_at, to = x, (x_up, x_down)[kind]
+        elif zq in (0, 3):
+            x_at, to = (x + 3) % 4, x_up
+        else:
+            x_at, to = (x + 1) % 4, x_down
+        ref = inv_part(zq, x_at)
+        return rdma(ref, ref, lx_send.at[kind, zq], lx_recv.at[kind, zq], to)
+
+    def lx_landed(kind, zq):
+        x_at = (x + (3, 1, 2)[kind]) % 4
+        landed(inv_part(zq, x_at), lx_send.at[kind, zq], lx_recv.at[kind, zq])
+
 
     own_slot = slot_of(y, col)
 
@@ -320,16 +278,11 @@
         y_copy(True, 1, p).start()
         y_copy(False, 1, p).start()
 
-    each(2, from_source)
-
     def assemble(m):
         own_b, own_f, other_b, other_f = columns(m)
         for k in range(RBK):
             front[k, m] = block(k, m, own_b, own_f, lambda n: got[n, other_b], other_f)
 
-    landed(got, pk_send.at[1], pk_recv.at[1])
-    each(RBK, assemble)
-
     def b_ready(p):
         @pl.when(holder)
         def _():
@@ -342,28 +295,16 @@
         x_copy(2, p).start()
         x_copy(3, p).start()
 
-    each(PIECES, b_ready)
-
     def from_pair(p):
         landed(right.at[s, own_slot, piece(2 * (1 - zl) + p)], pr_send.at[p], pr_recv.at[p])
         y_copy(True, 1, p + 2).start()
         y_copy(False, 1, p + 2).start()
-
-    each(2, from_pair)
-    hand_copy(0).start()
 
     def x_pass(p):
         x_landed(0, p)
         x_copy(4, p).start()
         x_landed(3, p)
         x_copy(5, p).start()
-
-    each(PIECES, x_pass)
-
-    lx_landed(0)
-    lx_copy(4).start()
-    lx_landed(3)
-    lx_copy(5).start()
 
     def y_pass(d):
         def go(q):
@@ -374,31 +315,9 @@
 
         return go
 
-    each(PIECES, y_pass(1))
-    hand_copy(1).start()
-    hand_copy(2).start()
-
-    each(RBK, lambda m: assemble(m + RBK))
-
     def x_rest(p):
         for which in (2, 1, 4, 5):
             x_landed(which, p)
-
-    each(PIECES, x_rest)
-    for which in (2, 1, 4, 5):
-        lx_landed(which)
-    inv_hand = rdma(inv.at[:, :, s], inv.at[:, :, s], lp_sem.at[0], lp_sem.at[1], mate)
-    inv_hand.start()
-
-    each(PIECES, y_pass(2))
-    hand_copy(3).start()
-    hand_copy(4).start()
-
-    landed(inv.at[:, :, other], lp_sem.at[0], lp_sem.at[1])
-    keep = lax.broadcasted_iota(jnp.int32, (256, 256), 0) >= lax.broadcasted_iota(jnp.int32, (256, 256), 1)
-    for nb in range(4):
-        tile = inv[nb, :, :, :, pl.ds(nb * 256, 256)].reshape(256, 256).astype(F32)
-        diag[nb] = jnp.where(keep, tile, 0.0).astype(BF16)
 
     def weights(nb):
         if nb == 0:
@@ -416,11 +335,6 @@
         y_landed(True, 3, q + 2)
         y_landed(False, 3, q + 2)
         y_copy(False, 4, q + 2).start()
-
-    each(2, y_last)
-    each(2, y_last2)
-    hand_copy(5).start()
-    hand_copy(6).start()
 
     def left_factor(t):
         part = pl.ds(pl.multiple_of(t * 320, 64), 320)
@@ -429,6 +343,101 @@
             fleft[part, pl.ds(nb * 256, 256)] = lax.dot_general(
                 lhs, weights(nb), NT, preferred_element_type=F32
             ).astype(BF16)
+
+    def inv_hand(zq, half):
+        ref = inv.at[zq, :, half, :, pl.ds(0, (zq + 1) * 256)]
+        return rdma(ref, ref, lp_send.at[zq], lp_recv.at[zq], mate)
+
+    def go_scatter(p):
+        scatter_copy(0, p).start()
+        scatter_copy(1, p).start()
+
+    def go_z(p):
+        z_copy(0, p).start()
+        z_copy(1, p).start()
+
+    def go_xa(p):
+        x_copy(0, p).start()
+        x_copy(1, p).start()
+
+    def relay_a(p):
+        a_here(p)
+        z_copy(2, p).start()
+        x_copy(0, p).start()
+        x_copy(1, p).start()
+
+    def panel():
+        own_b, own_f, other_b, other_f = columns(jnp.int32(0))
+        for k in range(RBK):
+            left[slot_a, pl.ds(k * BLK, BLK)] = block(k, 0, own_b, own_f, lambda n: got0[n], other_f)
+
+    @pl.when(holder)
+    def _():
+        panel()
+        each(2, go_scatter)
+        each(PIECES, go_z)
+        each(PIECES, go_xa)
+
+    landed(inv.at[z_below, x, s], lz_send.at[0], lz_recv.at[0])
+    lz_up2.start()
+    landed(inv.at[z_above, x, s], lz_send.at[1], lz_recv.at[1])
+    lz_down2.start()
+
+    @pl.when(jnp.logical_not(holder))
+    def _():
+        each(PIECES, relay_a)
+
+    each(2, from_source)
+
+    each(PIECES, b_ready)
+
+    each(2, from_pair)
+    hand_copy(0).start()
+
+    landed(far.at[pl.ds(0, 16)], lz_send.at[2], lz_recv.at[2])
+    landed(far.at[pl.ds(16, 16)], lz_send.at[3], lz_recv.at[3])
+    for zq in range(4):
+        lx_copy(0, zq).start()
+        lx_copy(1, zq).start()
+
+    landed(got, pk_send.at[1], pk_recv.at[1])
+    each(RBK, assemble)
+
+    each(PIECES, x_pass)
+
+    each(PIECES, y_pass(1))
+    hand_copy(1).start()
+    hand_copy(2).start()
+
+    for zq in range(4):
+        lx_landed(0 if zq in (0, 3) else 1, zq)
+        lx_copy(2, zq).start()
+
+    each(RBK, lambda m: assemble(m + RBK))
+
+    each(PIECES, y_pass(2))
+    hand_copy(3).start()
+    hand_copy(4).start()
+
+    each(PIECES, x_rest)
+
+    for zq in range(4):
+        lx_landed(1 if zq in (0, 3) else 0, zq)
+        lx_landed(2, zq)
+        inv_hand(zq, s).start()
+
+    each(2, y_last)
+    each(2, y_last2)
+    hand_copy(5).start()
+    hand_copy(6).start()
+
+    for zq in range(4):
+        landed(inv.at[zq, :, other, :, pl.ds(0, (zq + 1) * 256)], lp_send.at[zq], lp_recv.at[zq])
+    keep = lax.broadcasted_iota(jnp.int32, (256, 256), 0) >= lax.broadcasted_iota(jnp.int32, (256, 256), 1)
+    for nb in range(4):
+        tile = inv[nb, :, :, :, pl.ds(nb * 256, 256)].reshape(256, 256).astype(F32)
+        diag[nb] = jnp.where(keep, tile, 0.0).astype(BF16)
+
 
     each(2, left_factor)
 
@@ -475,10 +484,13 @@
 
     pk0_copy.wait_send()
     pk_copy.wait_send()
-    for copy in (lz_up, lz_down, lz_up2, lz_down2, inv_hand):
+    for copy in (lz_up, lz_down, lz_up2, lz_down2):
         copy.wait_send()
-    for which in range(6):
-        lx_copy(which).wait_send()
+    for zq in range(4):
+        inv_hand(zq, s).wait_send()
+    for kind in range(3):
+        for zq in range(4):
+            lx_copy(kind, zq).wait_send()
 
     @pl.when(holder)
     def _():
@@ -518,17 +530,19 @@
 def body(front_entries, block_pattern, child_update, child_map, diag_inverse):
     entries = front_entries.transpose(0, 4, 1, 2, 5, 3, 6).reshape(RBK, MB, BLK, BLK)
     child = child_update.transpose(0, 1, 4, 2, 5, 3, 6).reshape(CBK, CBK, BLK, BLK)
-    pattern = block_pattern.reshape(RBK, MB)
+    pattern = block_pattern.reshape(RBK, 1, MB)
     cmap = child_map.transpose(1, 0, 2)
-    smem = pl.BlockSpec(memory_space=pltpu.SMEM)
     anyspace = pl.BlockSpec(memory_space=pl.ANY)
+    hbm = pl.BlockSpec(memory_space=pltpu.HBM)
     dma = pltpu.SemaphoreType.DMA
     out = pl.pallas_call(
         kernel,
         out_shape=jax.ShapeDtypeStruct((RBK, MB, BLK, BLK), BF16),
-        in_specs=[smem, smem, anyspace, anyspace, anyspace],
+        in_specs=[hbm] * 5,
         out_specs=anyspace,
         scratch_shapes=[
+            pltpu.SMEM((CBK, 2, 16), jnp.int32),
+            pltpu.SMEM((RBK, 1, MB), jnp.int32),
             pltpu.VMEM((CBK, CBK, BLK, BLK), BF16),
             pltpu.VMEM((RBK, MB, BLK, BLK), BF16),
             pltpu.VMEM((RBK, MB, BLK, BLK), BF16),
@@ -543,11 +557,11 @@
             pltpu.VMEM((ROWS, PANEL), BF16),
             pltpu.VMEM((2 * BLK, PANEL), BF16),
             pltpu.VMEM((RBK, MB, BLK, BLK), BF16),
-            dma((3,)),
+            dma((5,)),
             dma((2,)), dma((2,)),
             dma((4,)), dma((4,)),
-            dma((6,)), dma((6,)),
-            dma((2,)),
+            dma((3, 4)), dma((3, 4)),
+            dma((4,)), dma((4,)),
             dma((2, 2)), dma((2,)),
             dma((2,)), dma((2,)),
             dma((2, PIECES)), dma((2, PIECES)),
@@ -557,7 +571,7 @@
             dma((RBK,)),
         ],
         compiler_params=pltpu.CompilerParams(
-            collective_id=0, has_side_effects=True, vmem_limit_bytes=48 * 1024 * 1024
+            collective_id=0, has_side_effects=True, vmem_limit_bytes=67043328
         ),
     )(cmap, pattern, entries, child, diag_inverse)
     out = out.reshape(RBK, MB, 1, 1, 1, BLK, BLK)

time: 73.8 us -> 61.6 us (0.83)
  Pallas kernels: 67.4 us -> 58.7 us
  local copies, waits for them, and re-layouts: 6.15 us -> 2.78 us
    pallas_call x1, Pallas kernels: 67.4 us -> 58.7 us  [body(): pl.pallas_call(kernel, out_shape=jax.ShapeDtypeStruct((RBK, MB, BLK, BLK)...]
    unnamed x10 -> x1, local copies, waits for them, and re-layouts: 6.15 us -> 2.78 us
where the time goes in v2:
time: 61.6 us; the launch traced here: 61.4 us
  Pallas kernels  58.7 us (95%)
  local copies, waits for them, and re-layouts  2.78 us (5%)
    pallas_call x1, Pallas kernels, body(): pl.pallas_call(kernel, out_shape=jax.ShapeDtypeStruct((RBK, MB, BLK, BLK)...  58.7 us
    unnamed x1, local copies, waits for them, and re-layouts  2.78 us

profile of v2, /device:TPU:1, one launch (start us, length us, event | category | flops | bytes accessed | tf_op | source)
XLA Modules:
  0.0 61.4 jit_solution(7667939767002050023)
XLA Ops:
  0.0 58.7 %shard_map.55 = bf16[5,10,128,128]{3,2,1,0:T(8,128)(2,1)} custom-call(s32[6,2,16]{2,1,0:T(2,128)} %bitcast.20, s32[5,1,10]{2,1,0:T(1,128)} %bitcast.21, bf16[5,10,128,128]{3,2,1,0:T(8,128)(2,1)} %bitcast.18, bf16[6,6,128,128]{3,2,1,0:T(8,128)(2,1)} %bitcast.19, bf16[64,1024]{1,0:T(8,128)(2,1)} %inverse_hbm.1), custom_call_target="tpu_custom_call" | custom-call | tf_op jit(solution)/shard_map/pallas_call | solution.py:538
  58.7 2.8 %copy.10 = bf16[5,1,1,128,10,1,128]{6,3,5,4,2,1,0:T(8,128)(2,1)} copy(bf16[5,1,1,128,10,1,128]{6,3,5,4,2,1,0:T(8,128)(2,1)} %bitcast.17) | data formatting | bytes 3276800

commit v3 on v2

--- a/solution.py
+++ b/solution.py
@@ -16,6 +16,7 @@
 ROWS = RBK * BLK
 PANEL = 1024
 PIECES = 4
+HALF = PIECES // 2
 PR = ROWS // PIECES
 NT = (((1,), (1,)), ((), ()))
 
@@ -25,12 +26,12 @@
 
 
 def kernel(
-    cmap_hbm, pattern_hbm, entries_hbm, child_hbm, inverse_hbm, out_hbm,
+    cmap_hbm, pattern_hbm, entries_hbm, child_hbm, inverse_hbm, outv,
     cmap, pattern,
-    child, entries, front, pack0, pack, got0, got, left, right, inv, diag, fleft, fright, outv,
+    child, entries, front, pack0, pack, got0, got, left, right, inv, diag, fleft, fright,
     local_sem, pk_send, pk_recv, lz_send, lz_recv, lx_send, lx_recv, lp_send, lp_recv,
     sc_send, sc_recv, pr_send, pr_recv, z_send, z_recv, x_send, x_recv,
-    y_send, y_recv, h_send, h_recv, out_sem,
+    y_send, y_recv, h_send, h_recv,
 ):
     s = lax.axis_index("sub")
     row = lax.axis_index("row")
@@ -150,7 +151,6 @@
     lz_down2 = rdma(high_half, high_half, lz_send.at[3], lz_recv.at[3], z_down)
 
     pk0_copy.start()
-    pk_copy.start()
 
     def block(k, m, own_b, own_f, theirs, theirs_f):
         a, have_a = own_at[k]
@@ -168,13 +168,14 @@
     pattern_in.wait()
     entries_in.wait()
     landed(got0, pk_send.at[0], pk_recv.at[0])
+    pk_copy.start()
 
     first = jnp.where((zh == 1) | (zh == 2), 1, 0)
     slot_a = first * 4 + x
     slot_b = (1 - first) * 4 + x
 
     def piece(p):
-        return pl.ds(pl.multiple_of(p * PR, 32), PR)
+        return pl.ds(pl.multiple_of(p * PR, 16), PR)
 
     def z_copy(which, p):
         ref = left.at[slot_a, piece(p)]
@@ -209,7 +210,7 @@
         landed(left.at[slot, piece(p)], x_send.at[which, p], x_recv.at[which, p])
 
     def scatter_copy(half, p):
-        part = piece(2 * half + p)
+        part = piece(HALF * half + p)
         return rdma(
             left.at[slot_a, part], right.at[s, slot_a, part], sc_send.at[half, p], sc_recv.at[p],
             {"row": send_y * 2 + half, "col": row},
@@ -241,7 +242,7 @@
     own_slot = slot_of(y, col)
 
     def turn(q):
-        return (2 * zl + q) % 4
+        return (HALF * zl + q) % PIECES
 
     def y_copy(up, d, q):
         slot = slot_of((y + 8 - (d - 1)) % 8 if up else (y + d - 1) % 8, col)
@@ -259,7 +260,7 @@
         )
 
     def pair_copy(p):
-        ref = right.at[s, own_slot, piece(2 * zl + p)]
+        ref = right.at[s, own_slot, piece(HALF * zl + p)]
         return rdma(ref, ref, pr_send.at[p], pr_recv.at[p], pair)
 
     def hand_copy(which):
@@ -269,11 +270,11 @@
 
     def hand_half(which):
         half = (zl + which) % 2
-        ref = right.at[s, slot_of((y + 4) % 8, col), pl.ds(pl.multiple_of(half * 2 * PR, 32), 2 * PR)]
+        ref = right.at[s, slot_of((y + 4) % 8, col), pl.ds(pl.multiple_of(half * HALF * PR, 16), HALF * PR)]
         return rdma(ref, ref, h_send.at[7 + which], h_recv.at[7 + which], mate)
 
     def from_source(p):
-        landed(right.at[s, own_slot, piece(2 * zl + p)], sc_send.at[0, p], sc_recv.at[p])
+        landed(right.at[s, own_slot, piece(HALF * zl + p)], sc_send.at[0, p], sc_recv.at[p])
         pair_copy(p).start()
         y_copy(True, 1, p).start()
         y_copy(False, 1, p).start()
@@ -296,9 +297,9 @@
         x_copy(3, p).start()
 
     def from_pair(p):
-        landed(right.at[s, own_slot, piece(2 * (1 - zl) + p)], pr_send.at[p], pr_recv.at[p])
-        y_copy(True, 1, p + 2).start()
-        y_copy(False, 1, p + 2).start()
+        landed(right.at[s, own_slot, piece(HALF * (1 - zl) + p)], pr_send.at[p], pr_recv.at[p])
+        y_copy(True, 1, p + HALF).start()
+        y_copy(False, 1, p + HALF).start()
 
     def x_pass(p):
         x_landed(0, p)
@@ -332,9 +333,9 @@
         y_landed(False, 3, q)
 
     def y_last2(q):
-        y_landed(True, 3, q + 2)
-        y_landed(False, 3, q + 2)
-        y_copy(False, 4, q + 2).start()
+        y_landed(True, 3, q + HALF)
+        y_landed(False, 3, q + HALF)
+        y_copy(False, 4, q + HALF).start()
 
     def left_factor(t):
         part = pl.ds(pl.multiple_of(t * 320, 64), 320)
@@ -374,7 +375,7 @@
     @pl.when(holder)
     def _():
         panel()
-        each(2, go_scatter)
+        each(HALF, go_scatter)
         each(PIECES, go_z)
         each(PIECES, go_xa)
 
@@ -387,11 +388,11 @@
     def _():
         each(PIECES, relay_a)
 
-    each(2, from_source)
+    each(HALF, from_source)
 
     each(PIECES, b_ready)
 
-    each(2, from_pair)
+    each(HALF, from_pair)
     hand_copy(0).start()
 
     landed(far.at[pl.ds(0, 16)], lz_send.at[2], lz_recv.at[2])
@@ -426,8 +427,8 @@
         lx_landed(2, zq)
         inv_hand(zq, s).start()
 
-    each(2, y_last)
-    each(2, y_last2)
+    each(HALF, y_last)
+    each(HALF, y_last2)
     hand_copy(5).start()
     hand_copy(6).start()
 
@@ -441,46 +442,45 @@
 
     each(2, left_factor)
 
-    each(2, lambda q: y_landed(True, 4, q))
+    each(HALF, lambda q: y_landed(True, 4, q))
     hand_half(0).start()
-    each(2, lambda q: y_landed(False, 4, q + 2))
+    each(HALF, lambda q: y_landed(False, 4, q + HALF))
     hand_half(1).start()
+
+    def right_factor(half):
+        def go(t):
+            part = pl.ds(pl.multiple_of(t * 320, 64), 320)
+            for nb in range(4):
+                lhs = jnp.concatenate([right[half, c, part] for c in range(2 * nb + 2)], axis=1)
+                fright[half, part, pl.ds(nb * 256, 256)] = lax.dot_general(
+                    lhs, weights(nb), NT, preferred_element_type=F32
+                ).astype(BF16)
+
+        return go
+
+    each(2, right_factor(s))
 
     for which, shift in enumerate([0, 7, 1, 6, 2, 5, 3]):
         landed(right.at[other, slot_of((y + shift) % 8, col)], h_send.at[which], h_recv.at[which])
     for which in range(2):
         half = (zl + which) % 2
         landed(
-            right.at[other, slot_of((y + 4) % 8, col), pl.ds(pl.multiple_of(half * 2 * PR, 32), 2 * PR)],
+            right.at[other, slot_of((y + 4) % 8, col), pl.ds(pl.multiple_of(half * HALF * PR, 16), HALF * PR)],
             h_send.at[7 + which], h_recv.at[7 + which],
         )
 
-    def out_copy(kk):
-        cols = pl.ds(2 * kk, 2)
-        return pltpu.make_async_copy(outv.at[:, cols], out_hbm.at[:, cols], out_sem.at[kk])
+    each(2, right_factor(other))
 
     def finish(kk):
         part = pl.ds(pl.multiple_of(kk * BLK, BLK), BLK)
-        for nb in range(4):
-            lhs = jnp.concatenate(
-                [
-                    jnp.concatenate([right[h, c, part] for c in range(2 * nb + 2)], axis=1)
-                    for h in range(2)
-                ],
-                axis=0,
-            )
-            fright[:, pl.ds(nb * 256, 256)] = lax.dot_general(
-                lhs, weights(nb), NT, preferred_element_type=F32
-            ).astype(BF16)
-        product = lax.dot_general(fleft[...], fright[...], NT, preferred_element_type=F32)
+        both = jnp.concatenate([fright[0, part], fright[1, part]], axis=0)
+        product = lax.dot_general(fleft[...], both, NT, preferred_element_type=F32)
         for k in range(RBK):
             for h in range(2):
                 tile = product[k * BLK:(k + 1) * BLK, h * BLK:(h + 1) * BLK]
                 outv[k, 2 * kk + h] = (front[k, 2 * kk + h].astype(F32) - tile).astype(BF16)
-        out_copy(kk).start()
 
     each(RBK, finish)
-    each(RBK, lambda kk: out_copy(kk).wait())
 
     pk0_copy.wait_send()
     pk_copy.wait_send()
@@ -498,7 +498,7 @@
             scatter_copy(0, p).wait_send()
             scatter_copy(1, p).wait_send()
 
-        each(2, done)
+        each(HALF, done)
 
     def left_done(p):
         z_copy(0, p).wait_send()
@@ -518,9 +518,9 @@
     def last_done(p):
         pair_copy(p).wait_send()
         y_copy(True, 4, p).wait_send()
-        y_copy(False, 4, p + 2).wait_send()
-
-    each(2, last_done)
+        y_copy(False, 4, p + HALF).wait_send()
+
+    each(HALF, last_done)
     for which in range(7):
         hand_copy(which).wait_send()
     for which in range(2):
@@ -532,14 +532,16 @@
     child = child_update.transpose(0, 1, 4, 2, 5, 3, 6).reshape(CBK, CBK, BLK, BLK)
     pattern = block_pattern.reshape(RBK, 1, MB)
     cmap = child_map.transpose(1, 0, 2)
-    anyspace = pl.BlockSpec(memory_space=pl.ANY)
     hbm = pl.BlockSpec(memory_space=pltpu.HBM)
     dma = pltpu.SemaphoreType.DMA
+    entries, child, pattern, cmap, diag_inverse = (
+        pltpu.with_memory_space_constraint(v, pltpu.HBM) for v in (entries, child, pattern, cmap, diag_inverse)
+    )
     out = pl.pallas_call(
         kernel,
         out_shape=jax.ShapeDtypeStruct((RBK, MB, BLK, BLK), BF16),
         in_specs=[hbm] * 5,
-        out_specs=anyspace,
+        out_specs=pl.BlockSpec(memory_space=pltpu.VMEM),
         scratch_shapes=[
             pltpu.SMEM((CBK, 2, 16), jnp.int32),
             pltpu.SMEM((RBK, 1, MB), jnp.int32),
@@ -555,23 +557,21 @@
             pltpu.VMEM((4, 4, 2, 32, PANEL), BF16),
             pltpu.VMEM((4, 256, 256), BF16),
             pltpu.VMEM((ROWS, PANEL), BF16),
-            pltpu.VMEM((2 * BLK, PANEL), BF16),
-            pltpu.VMEM((RBK, MB, BLK, BLK), BF16),
+            pltpu.VMEM((2, ROWS, PANEL), BF16),
             dma((5,)),
             dma((2,)), dma((2,)),
             dma((4,)), dma((4,)),
             dma((3, 4)), dma((3, 4)),
             dma((4,)), dma((4,)),
-            dma((2, 2)), dma((2,)),
-            dma((2,)), dma((2,)),
+            dma((2, HALF)), dma((HALF,)),
+            dma((HALF,)), dma((HALF,)),
             dma((2, PIECES)), dma((2, PIECES)),
             dma((6, PIECES)), dma((6, PIECES)),
             dma((2, 4, PIECES)), dma((2, 4, PIECES)),
             dma((9,)), dma((9,)),
-            dma((RBK,)),
         ],
         compiler_params=pltpu.CompilerParams(
-            collective_id=0, has_side_effects=True, vmem_limit_bytes=67043328
+            collective_id=0, has_side_effects=True, vmem_limit_bytes=52000000
         ),
     )(cmap, pattern, entries, child, diag_inverse)
     out = out.reshape(RBK, MB, 1, 1, 1, BLK, BLK)

time: 61.6 us -> 58.5 us (0.950)
  local copies, waits for them, and re-layouts: 2.78 us -> 1.17 us
  Pallas kernels: 58.7 us -> 57.2 us
    unnamed x1, local copies, waits for them, and re-layouts: 2.78 us -> 1.17 us
    pallas_call x1, Pallas kernels: 58.7 us -> 57.2 us  [body(): pl.pallas_call(kernel, out_shape=jax.ShapeDtypeStruct((RBK, MB, BLK, BLK)...]
where the time goes in v3:
time: 58.5 us; the launch traced here: 58.4 us
  Pallas kernels  57.2 us (98%)
  local copies, waits for them, and re-layouts  1.17 us (2%)
    pallas_call x1, Pallas kernels, body(): pl.pallas_call(kernel, out_shape=jax.ShapeDtypeStruct((RBK, MB, BLK, BLK)...  57.2 us

profile of v3, /device:TPU:1, one launch (start us, length us, event | category | flops | bytes accessed | tf_op | source)
XLA Modules:
  0.0 58.4 jit_solution(18177824065476326465)
XLA Ops:
  0.0 57.2 %shard_map.55 = bf16[5,10,128,128]{3,2,1,0:T(8,128)(2,1)S(1)} custom-call(s32[6,2,16]{2,1,0:T(2,128)} %bitcast.20, s32[5,1,10]{2,1,0:T(1,128)} %bitcast.21, bf16[5,10,128,128]{3,2,1,0:T(8,128)(2,1)} %bitcast.18, bf16[6,6,128,128]{3,2,1,0:T(8,128)(2,1)} %bitcast.19, bf16[64,1024]{1,0:T(8,128)(2,1)} %inverse_hbm.1), custom_call_target="tpu_custom_call" | custom-call | tf_op jit(solution)/shard_map/pallas_call | solution.py:540
  57.2 1.2 %copy.10 = bf16[5,1,1,128,10,1,128]{6,3,5,4,2,1,0:T(8,128)(2,1)} copy(bf16[5,1,1,128,10,1,128]{6,3,5,4,2,1,0:T(8,128)(2,1)S(1)} %bitcast.17) | data formatting | bytes 3276800
